TPU v7x, 512 devices: a whole 4x4x16 slice. The times are simulated.
512 devices in a mesh: req: 8 (over x, core), vocab: 64 (over y, z).
Axes of the slice: x: 4, y: 4, z: 16, core: 2. Of those that a mesh axis runs over, the one named last changes fastest.
Arguments:
- hidden: bfloat16 [8192, 2304], P(('req', 'vocab'))
- norm_gain: float32 [2304], replicated, may hold values from 0.5 to 1.5
- head_weight: bfloat16 [2304, 65536], P(None, 'vocab')
- targets: int32 [8192], P(('req', 'vocab')), may hold values from 0 to 65535
- counts: int32 [512], P(('req', 'vocab')), may hold values from 5 to 10, as said below
Outputs:
- logprob: float32 [8192], P(('req', 'vocab'))
- entropy: float32 [8192], P(('req', 'vocab'))
Inputs may be any that keep to these rules, and one draw needn't show every extreme that they name: The scored slots of a device are its first counts slots; some device holds exactly 10.
All inputs are finite; a program needn't handle non-finite values.
Results may differ from a plain program's by a relative error of at most 0.012.
The roundings to bfloat16 on the way count: a program that leaves them out, or rounds other values in their place, can miss the bound.
Values may be sent and summed in bfloat16 or wider, within the bound.
A program may use at most 64 MiB of HBM per device.

v0:
```python
import jax
import jax.numpy as jnp
from jax import lax
from jax.sharding import PartitionSpec as P

logit_scale = 256.0 / 2304.0


def on_device(hidden, norm_gain, head_weight, targets, counts):
    slots = hidden.shape[0]
    vocab_dev = head_weight.shape[1]
    values = hidden.astype(jnp.float32)
    square_mean = jnp.mean(values * values, axis=1, keepdims=True)
    normed = (values * lax.rsqrt(square_mean + 1e-05) * norm_gain[None, :]).astype(jnp.bfloat16)
    gathered = lax.all_gather(normed, "vocab", axis=0, tiled=True)
    wanted = lax.all_gather(targets, "vocab", axis=0, tiled=True)
    position = lax.axis_index("vocab")
    start = position * vocab_dev
    logits = jnp.dot(gathered, head_weight, preferred_element_type=jnp.float32) * logit_scale
    local_peak = jnp.max(logits, axis=1)
    weights = jnp.exp(logits - local_peak[:, None])
    local_total = jnp.sum(weights, axis=1)
    local_moment = jnp.sum(weights * logits, axis=1)
    columns = lax.broadcasted_iota(jnp.int32, logits.shape, 1)
    hits = columns == (wanted - start)[:, None]
    local_chosen = jnp.sum(jnp.where(hits, logits, jnp.float32(0.0)), axis=1)
    own_start = position * slots
    peak = lax.pmax(local_peak, "vocab")
    factor = jnp.exp(local_peak - peak)
    total, moment, chosen = lax.psum(
        (local_total * factor, local_moment * factor, local_chosen), "vocab"
    )
    peak = lax.dynamic_slice_in_dim(peak, own_start, slots, 0)
    total = lax.dynamic_slice_in_dim(total, own_start, slots, 0)
    moment = lax.dynamic_slice_in_dim(moment, own_start, slots, 0)
    chosen = lax.dynamic_slice_in_dim(chosen, own_start, slots, 0)
    log_total = jnp.log(total)
    row_logprob = chosen - peak - log_total
    row_entropy = peak + log_total - moment / total
    scored = jnp.arange(slots, dtype=jnp.int32) < counts[0]
    logprob = jnp.where(scored, row_logprob, jnp.float32(0.0))
    entropy = jnp.where(scored, row_entropy, jnp.float32(0.0))
    return (logprob, entropy)


def solution(mesh):
    in_specs = (
        P(("req", "vocab"), None),
        P(),
        P(None, "vocab"),
        P(("req", "vocab")),
        P(("req", "vocab")),
    )
    out_specs = (P(("req", "vocab")), P(("req", "vocab")))
    return jax.shard_map(
        on_device, mesh=mesh, in_specs=in_specs, out_specs=out_specs, check_vma=False
    )
```

profile of v0, /device:TPU:2, one launch (start us, length us, event | category | flops | bytes accessed | tf_op | source)
XLA Modules:
  0.0 597.7 jit_solution(12411785864831970918)
XLA Ops:
  7.2 0.0 all-gather.2.cloned.1.call-start
  7.2 1.0 fusion.1
  8.2 1.6 fusion.3
  9.8 0.0 all-gather.2.cloned.1.call-update
  10.5 1.3 dynamic-slice
  12.5 0.9 dynamic-update-slice
  13.3 34.4 %all-reduce = s32[1024]{0:T(1024)S(1)} all-reduce(s32[1024]{0:T(1024)S(1)} %dynamic-update-slice), channel_id=1, replica_groups=mesh['req'=8,'vocab'=64] {'vocab'}, use_global_device_ids=true, to_apply=%add | all-reduce | flops 1024 | bytes 8192
  47.7 115.1 %all-gather.2.cloned.1.call-done = bf16[1024,2304]{1,0:T(8,128)(2,1)} async-done(((bf16[16,2304]{1,0:T(8,128)(2,1)}), bf16[1024,2304]{1,0:T(8,128)(2,1)}) %all-gather.2.cloned.1.call-update) | async-done | bytes 4718608 | tf_op jit(solution)/shard_map/all_gather | solution.py:15
  162.8 9.8 %multiply_reduce_fusion.1 = (f32[1024]{0:T(1024)S(1)}, f32[1024,1024]{0,1:T(8,128)}) fusion(bf16[1024,2304]{1,0:T(8,128)(2,1)} %all-gather.2.cloned.1.call-done, bf16[2304,1024]{1,0:T(8,128)(2,1)} %param.7), kind=kOutput, calls=%fused_computation.5 | convolution fusion | flops 4833934336 | bytes 13635584 | tf_op jit(solution)/shard_map/dot_general | solution.py:19
  172.6 140.0 %pmax.7 = f32[1024]{0:T(1024)S(1)} all-reduce(f32[1024]{0:T(1024)S(1)} %get-tuple-element.12), channel_id=1, replica_groups=mesh['req'=8,'vocab'=64] {'vocab'}, use_global_device_ids=true, to_apply=%region_4.5 | all-reduce | flops 1024 | bytes 8192 | tf_op jit(solution)/shard_map/pmax | solution.py:28
  312.6 3.7 multiply_reduce_fusion
  316.3 274.0 %all-reduce.1 = (f32[1024]{0:T(1024)S(1)}, f32[1024]{0:T(1024)S(1)}, f32[1024]{0:T(1024)S(1)}) all-reduce(f32[1024]{0:T(1024)S(1)} %get-tuple-element.4, f32[1024]{0:T(1024)S(1)} %get-tuple-element.11, f32[1024]{0:T(1024)S(1)} %get-tuple-element.10), channel_id=1, replica_groups=mesh['req'=8,'vocab'=64] {'vocab'}, use_global_device_ids=true, to_apply=%region_2.0 | all-reduce | flops 3072 | bytes 24576 | tf_op jit(solution)/shard_map/psum | solution.py:30
  590.3 0.6 compare_select_fusion
  (4 shorter events, 0.0 us)
Async XLA Ops:
  7.2 155.7 %all-gather.2.cloned.1.call-start = ((), (), s32[]{:S(2)}) async-start(), calls=%async_computation | async-start | bytes 4792320 | tf_op jit(solution)/shard_map/all_gather | solution.py:15
Sparse Core Ops, SparseCore 0:
  10.9 151.8 all-gather.1
where the time goes:
time: 598 us
  blocking collectives  448 us (75%)
  waiting for transfers between devices  115 us (19%)
  between operations  15.4 us (3%)
  matrix products  9.76 us (2%)
  other arithmetic  6.94 us (1%)
    psum x1, blocking collectives, on_device(): lax.psum((local_total * factor, local_moment * factor, local_chosen), 'vo...  274 us
    pmax x1, blocking collectives, on_device(): peak = lax.pmax(local_peak, 'vocab')  140 us
    all_gather x1, waiting for transfers between devices, on_device(): gathered = lax.all_gather(normed, 'vocab', axis=0, tiled=True)  115 us
    unnamed x1, blocking collectives  34.4 us
  transfers between devices with their start and end apart: 1, of which 1 were waited for; matrix products, arithmetic and copies ran while one was open for 0% of the time, Pallas kernels for 0%

commit v1 on v0

--- a/solution.py
+++ b/solution.py
@@ -12,7 +12,10 @@
     values = hidden.astype(jnp.float32)
     square_mean = jnp.mean(values * values, axis=1, keepdims=True)
     normed = (values * lax.rsqrt(square_mean + 1e-05) * norm_gain[None, :]).astype(jnp.bfloat16)
-    gathered = lax.all_gather(normed, "vocab", axis=0, tiled=True)
+    gathered = jnp.concatenate(
+        jax.lax.all_to_all(jnp.stack(jax.lax.axis_size("vocab") * [normed], axis=0), "vocab", 0, 0),
+        axis=0,
+    )
     wanted = lax.all_gather(targets, "vocab", axis=0, tiled=True)
     position = lax.axis_index("vocab")
     start = position * vocab_dev

time: 598 us -> 678 us (1.13)
  the two profiles are of different devices: /device:TPU:2 before, /device:TPU:6 now
where the time goes in v1:
time: 678 us
  blocking collectives  637 us (94%)
  starting transfers between devices  19.1 us (3%)
  matrix products  9.77 us (1%)
    psum x1, blocking collectives, on_device(): lax.psum((local_total * factor, local_moment * factor, local_chosen), 'vo...  274 us
    unnamed x1, blocking collectives  222 us
    pmax x1, blocking collectives, on_device(): peak = lax.pmax(local_peak, 'vocab')  141 us
    all_to_all x1, starting transfers between devices, on_device(): jax.lax.all_to_all(jnp.stack(jax.lax.axis_size('vocab') * [normed], axis=...  19.1 us
  transfers between devices with their start and end apart: 1, of which 0 were waited for; matrix products, arithmetic and copies ran while one was open for 0% of the time, Pallas kernels for 0%

profile of v1, /device:TPU:6, one launch (start us, length us, event | category | flops | bytes accessed | tf_op | source)
XLA Modules:
  0.0 677.8 jit_solution(18378045166115038585)
XLA Ops:
  0.6 1.0 fusion.1
  1.7 1.0 fusion.3
  2.6 2.5 stack.2
  5.1 0.0 copy-start
  5.1 19.1 %all-to-all-start = ((bf16[64,16,2304]{2,1,0:T(8,128)(2,1)}), bf16[64,16,2304]{2,1,0:T(8,128)(2,1)}, u32[]{:S(2)}, u32[]{:S(2)}) async-start(bf16[64,16,2304]{2,1,0:T(8,128)(2,1)} %stack.2), calls=%async_computation | async-start | bytes 9437184 | tf_op jit(solution)/shard_map/all_to_all | solution.py:16
  24.9 1.3 dynamic-slice
  26.8 0.0 copy-done
  26.8 0.2 dynamic-update-slice
  27.1 221.6 %all-reduce = s32[1024]{0:T(1024)S(1)} all-reduce(s32[1024]{0:T(1024)S(1)} %dynamic-update-slice), channel_id=1, replica_groups=mesh['req'=8,'vocab'=64] {'vocab'}, use_global_device_ids=true, to_apply=%add | all-reduce | flops 1024 | bytes 8192
  248.6 0.0 all-to-all-done
  248.6 9.8 %multiply_reduce_fusion.1 = (f32[1024]{0:T(1024)S(1)}, f32[1024,1024]{0,1:T(8,128)}) fusion(bf16[1024,2304]{1,0:T(8,128)(2,1)} %bitcast.2, bf16[2304,1024]{1,0:T(8,128)(2,1)} %param.7), kind=kOutput, calls=%fused_computation.5 | convolution fusion | flops 4833934336 | bytes 13635584 | tf_op jit(solution)/shard_map/dot_general | solution.py:22
  258.4 141.1 %pmax.7 = f32[1024]{0:T(1024)S(1)} all-reduce(f32[1024]{0:T(1024)S(1)} %get-tuple-element.12), channel_id=1, replica_groups=mesh['req'=8,'vocab'=64] {'vocab'}, use_global_device_ids=true, to_apply=%region_4.5 | all-reduce | flops 1024 | bytes 8192 | tf_op jit(solution)/shard_map/pmax | solution.py:31
  399.5 3.7 multiply_reduce_fusion
  403.2 274.0 %all-reduce.1 = (f32[1024]{0:T(1024)S(1)}, f32[1024]{0:T(1024)S(1)}, f32[1024]{0:T(1024)S(1)}) all-reduce(f32[1024]{0:T(1024)S(1)} %get-tuple-element.4, f32[1024]{0:T(1024)S(1)} %get-tuple-element.11, f32[1024]{0:T(1024)S(1)} %get-tuple-element.10), channel_id=1, replica_groups=mesh['req'=8,'vocab'=64] {'vocab'}, use_global_device_ids=true, to_apply=%region_2.0 | all-reduce | flops 3072 | bytes 24576 | tf_op jit(solution)/shard_map/psum | solution.py:33
  677.2 0.6 compare_select_fusion
  (4 shorter events, 0.0 us)
Async XLA Ops:
  5.1 21.7 %copy-start = (s32[16]{0:T(128)S(1)}, s32[16]{0:T(128)}, u32[]{:S(2)}) copy-start(s32[16]{0:T(128)} %param.8) | copy-start | bytes 196
  5.1 243.5 %all-to-all-start = ((bf16[64,16,2304]{2,1,0:T(8,128)(2,1)}), bf16[64,16,2304]{2,1,0:T(8,128)(2,1)}, u32[]{:S(2)}, u32[]{:S(2)}) async-start(bf16[64,16,2304]{2,1,0:T(8,128)(2,1)} %stack.2), calls=%async_computation | async-start | bytes 9437184 | tf_op jit(solution)/shard_map/all_to_all | solution.py:16
